TPU v7x, 32 devices: a whole 2x2x4 slice. The times are simulated.
32 devices in a mesh: section: 8 (over y, x, core), tensor: 4 (over z).
Axes of the slice: x: 2, y: 2, z: 4, core: 2. Of those that a mesh axis runs over, the one named last changes fastest.
Arguments:
- acts: bfloat16 [8, 2, 32, 4096], P('section', None, None, 'tensor'), may hold values from -6 to 6
- grads_in: bfloat16 [8, 2, 32, 4096], P('section', None, None, 'tensor'), may hold values from -6 to 6
- head_grads: bfloat16 [8, 2, 128, 512], P('section', None, None, 'tensor'), may hold values from -6 to 6
- types: int32 [8, 2, 32], P('section'), may hold values 0 or 1
- gains: bfloat16 [8, 2, 2, 1024], P('section'), may hold values from 0.3984375 to 1.59375
- w_query: bfloat16 [8, 2, 4096, 512], P('section', None, None, 'tensor'), may hold values from -0.09375 to 0.09375
- w_key: bfloat16 [8, 2, 4096, 128], P('section', None, None, 'tensor'), may hold values from -0.09375 to 0.09375
- w_value: bfloat16 [8, 2, 4096, 128], P('section', None, None, 'tensor'), may hold values from -0.09375 to 0.09375
Outputs:
- routed: bfloat16 [8, 2, 32, 4096], P('section', None, None, 'tensor')
All inputs are finite; a program needn't handle non-finite values. No bound on the sum of `types` on one device may be relied on, other than what follows from the above.
Results may differ from a plain program's by a relative error of at most 0.0055.
Values may be sent and summed in bfloat16 or wider, within the bound.
A program may use at most 64 MiB of HBM per device.

v0:
```python
import jax
import jax.numpy as jnp
from jax import lax
from jax.sharding import PartitionSpec as P

HEAD_DIM = 128
SUB = 4
epsilon = 1e-05


def swapped(value, axis, stride):
    mask = 2**stride
    pairs = [(source, source ^ mask) for source in range(lax.axis_size(axis))]
    return lax.ppermute(value, axis, pairs)


def shifted(value, axis, by):
    peers = lax.axis_size(axis)
    return lax.ppermute(value, axis, [(i, (i + by) % peers) for i in range(peers)])


def sum_columns(first, second):
    return (
        lax.psum_scatter(first, "tensor", scatter_dimension=2, tiled=True),
        lax.psum_scatter(second, "tensor", scatter_dimension=2, tiled=True),
    )


def collect_rows(member, position, levels, axis):
    for bit in range(levels):
        partner = swapped(member, "section", bit)
        upper_bit = position >> bit & 1
        member = jnp.where(
            upper_bit == 1,
            jnp.concatenate([partner, member], axis=axis),
            jnp.concatenate([member, partner], axis=axis),
        )
    return member


def halve_once(member, upper_bit, bit):
    half_rows = member.shape[1] // 2
    lower_rows = member[:, :half_rows]
    higher_rows = member[:, half_rows:]
    kept_rows = jnp.where(upper_bit == 1, higher_rows, lower_rows)
    sent_rows = jnp.where(upper_bit == 1, lower_rows, higher_rows)
    return kept_rows + swapped(sent_rows, "section", bit)


def reduce_rows(first, second, position, levels):
    for bit in reversed(range(levels)):
        upper_bit = position >> bit & 1
        first = halve_once(first, upper_bit, bit)
        second = halve_once(second, upper_bit, bit)
    return (first, second)


def per_device(acts, grads_in, head_grads, types, gains, w_query, w_key, w_value):
    tensors = lax.axis_size("tensor")
    section_count = lax.axis_size("section") // SUB
    levels = SUB.bit_length() - 1
    position = lax.axis_index("section") % SUB
    section_here = lax.axis_index("section") // SUB
    x_local = acts[0]
    grad_local = grads_in[0]
    out_grads = head_grads[0]
    w_query = w_query[0]
    w_key = w_key[0]
    w_value = w_value[0]
    x_cols = lax.all_gather(x_local, "tensor", axis=2, tiled=True)
    x_full = collect_rows(x_cols, position, levels, 1)
    kind_full = collect_rows(types[0].astype(jnp.bfloat16), position, levels, 1)
    gain_full = collect_rows(gains[0], position, levels, 2).astype(jnp.float32)
    tokens = x_full.shape[1]
    tokq = x_local.shape[1]
    width = x_full.shape[2]
    cols_dev = x_local.shape[2]
    x_float = x_full.astype(jnp.float32)
    inverse = lax.rsqrt(jnp.mean(x_float * x_float, axis=-1, keepdims=True) + epsilon)
    gain_rows = jnp.where(kind_full[..., None] > 0.5, gain_full[:, 1:2, :], gain_full[:, 0:1, :])
    normed = (x_float * inverse * gain_rows).astype(jnp.bfloat16)
    queries = jnp.einsum(
        "ctd,cdh->cth", normed, w_query, preferred_element_type=jnp.float32
    ).astype(jnp.bfloat16)
    key_part = jnp.einsum("ctd,cdh->cth", normed, w_key, preferred_element_type=jnp.float32).astype(
        jnp.bfloat16
    )
    value_part = jnp.einsum(
        "ctd,cdh->cth", normed, w_value, preferred_element_type=jnp.float32
    ).astype(jnp.bfloat16)
    key_rows, value_rows = (
        lax.all_gather(key_part, "tensor", axis=2, tiled=True),
        lax.all_gather(value_part, "tensor", axis=2, tiled=True),
    )
    softmax_scale = HEAD_DIM ** (-0.5)
    scores = (
        jnp.einsum("cqh,ckh->cqk", queries, key_rows, preferred_element_type=jnp.float32)
        * softmax_scale
    )
    causal = jnp.arange(tokens)[:, None] >= jnp.arange(tokens)[None, :]
    scores = jnp.where(causal[None], scores, -1e30)
    attn_probs = jax.nn.softmax(scores, axis=-1)
    probs_low = attn_probs.astype(jnp.bfloat16)
    prob_grads = jnp.einsum(
        "cqh,ckh->cqk", out_grads, value_rows, preferred_element_type=jnp.float32
    )
    score_grads = (
        attn_probs
        * (prob_grads - jnp.sum(prob_grads * attn_probs, axis=-1, keepdims=True))
        * softmax_scale
    ).astype(jnp.bfloat16)
    query_grads = jnp.einsum(
        "cqk,ckh->cqh", score_grads, key_rows, preferred_element_type=jnp.float32
    ).astype(jnp.bfloat16)
    key_each = jnp.einsum("cqk,cqh->ckh", score_grads, queries, preferred_element_type=jnp.float32)
    value_each = jnp.einsum(
        "cqk,cqh->ckh", probs_low, out_grads, preferred_element_type=jnp.float32
    )
    key_sum, value_sum = sum_columns(key_each, value_each)
    key_grads = key_sum.astype(jnp.bfloat16)
    value_grads = value_sum.astype(jnp.bfloat16)
    joined_grads = jnp.concatenate([query_grads, key_grads, value_grads], axis=2)
    joined_weights = jnp.concatenate([w_query, w_key, w_value], axis=2)
    partial_value = jnp.einsum(
        "cth,cdh->ctd", joined_grads, joined_weights, preferred_element_type=jnp.float32
    )
    stat_part = jnp.sum(x_float * gain_rows * partial_value, axis=-1)
    stat_wide = jnp.broadcast_to(stat_part[..., None], stat_part.shape + (tensors,))
    grad_rows_sum, stat_rows = reduce_rows(partial_value, stat_wide, position, levels)
    grad_mine, stat_mine = sum_columns(grad_rows_sum, stat_rows)
    my_inverse = lax.dynamic_slice_in_dim(inverse, position * tokq, tokq, 1)
    my_gain = lax.dynamic_slice_in_dim(gain_rows, position * tokq, tokq, 1)
    my_gain = lax.dynamic_slice_in_dim(my_gain, lax.axis_index("tensor") * cols_dev, cols_dev, 2)
    my_x = x_local.astype(jnp.float32)
    stat_mean = stat_mine / width
    norm_grads = my_inverse * my_gain * grad_mine - my_x * my_inverse**3 * stat_mean
    result = (grad_local.astype(jnp.float32) + norm_grads).astype(jnp.bfloat16)
    arrived = shifted(result, "section", -SUB)
    routed = jnp.where(section_here == section_count - 1, arrived[::-1], arrived)
    return routed[None]


def solution(mesh):
    return jax.shard_map(
        per_device,
        mesh=mesh,
        in_specs=(
            P("section", None, None, "tensor"),
            P("section", None, None, "tensor"),
            P("section", None, None, "tensor"),
            P("section", None, None),
            P("section", None, None, None),
            P("section", None, None, "tensor"),
            P("section", None, None, "tensor"),
            P("section", None, None, "tensor"),
        ),
        out_specs=P("section", None, None, "tensor"),
        check_vma=False,
    )
```

profile of v0, /device:TPU:0, one launch (start us, length us, event | category | flops | bytes accessed | tf_op | source)
XLA Modules:
  0.0 225.5 jit_solution(11091461946398277763)
XLA Ops:
  7.8 17.7 %all-gather = bf16[1,2,32,4096]{3,2,1,0:T(8,128)(2,1)S(1)} all-gather(bf16[1,2,32,1024]{3,2,1,0:T(8,128)(2,1)} %param.8), channel_id=2, replica_groups=mesh['section'=8,'tensor'=4] {'tensor'}, dimensions={3}, use_global_device_ids=true | all-gather | bytes 655360 | tf_op jit(solution)/shard_map/all_gather | solution.py:70
  25.6 1.5 collective-permute-start.3
  29.2 2.4 %collective-permute-done.5 = bf16[2,2,2048]{2,1,0:T(2,128)(2,1)S(1)} collective-permute-done((bf16[2,2,2048]{2,1,0:T(2,128)(2,1)S(1)}, bf16[2,2,2048]{2,1,0:T(2,128)(2,1)S(1)}, u32[]{:S(2)}, u32[]{:S(2)}) %collective-permute-start.5) | collective-permute-done | bytes 16416 | tf_op jit(solution)/shard_map/ppermute | solution.py:14
  32.7 23.5 %collective-permute-done.1 = bf16[2,64,4096]{2,1,0:T(8,128)(2,1)S(1)} collective-permute-done((bf16[2,64,4096]{2,1,0:T(8,128)(2,1)S(1)}, bf16[2,64,4096]{2,1,0:T(8,128)(2,1)S(1)}, u32[]{:S(2)}, u32[]{:S(2)}) %collective-permute-start.1) | collective-permute-done | bytes 1048608 | tf_op jit(solution)/shard_map/ppermute | solution.py:14
  57.0 1.3 convolution_convert_fusion.2
  58.2 13.4 %all_gather.10 = bf16[2,128,128]{1,2,0:T(8,128)(2,1)S(1)} all-gather(bf16[2,128,32]{1,2,0:T(8,128)(2,1)S(1)} %convolution_convert_fusion.2), channel_id=1, replica_groups=mesh['section'=8,'tensor'=4] {'tensor'}, dimensions={2}, use_global_device_ids=true | all-gather | bytes 81920 | tf_op jit(solution)/shard_map/all_gather | solution.py:92
  71.7 1.3 convolution_convert_fusion.1
  72.9 13.2 %all_gather.11 = bf16[2,128,128]{1,2,0:T(8,128)(2,1)S(1)} all-gather(bf16[2,128,32]{1,2,0:T(8,128)(2,1)S(1)} %convolution_convert_fusion.1), channel_id=1, replica_groups=mesh['section'=8,'tensor'=4] {'tensor'}, dimensions={2}, use_global_device_ids=true | all-gather | bytes 81920 | tf_op jit(solution)/shard_map/all_gather | solution.py:93
  86.2 1.4 fusion.22
  89.6 1.9 fusion.25
  91.6 2.8 %copy.11 = bf16[1,2,4096,128]{2,3,1,0:T(8,128)(2,1)} copy(bf16[1,2,4096,128]{3,2,1,0:T(8,128)(2,1)S(1)} %copy-done.1) | data formatting | bytes 4194304 | tf_op args[5]
  95.6 13.9 %reduce-scatter.6.cloned.1.call-done = f32[2,128,32]{1,2,0:T(8,128)} async-done(((f32[2,128,128]{1,2,0:T(8,128)}), f32[2,128,32]{1,2,0:T(8,128)}) %reduce-scatter.6.cloned.1.call-update) | async-done | bytes 32784 | tf_op jit(solution)/shard_map/reduce_scatter | solution.py:25
  110.2 19.1 %reduce-scatter.4.cloned.1.call-done = f32[2,128,32]{1,2,0:T(8,128)} async-done(((f32[2,128,128]{1,2,0:T(8,128)}), f32[2,128,32]{1,2,0:T(8,128)}) %reduce-scatter.4.cloned.1.call-update) | async-done | bytes 32784 | tf_op jit(solution)/shard_map/reduce_scatter | solution.py:24
  130.1 5.5 %fusion.6 = (f32[2,128]{1,0:T(2,128)S(1)}, f32[2,128,4096]{2,1,0:T(8,128)}, f32[2,128,4096]{2,1,0:T(8,128)S(1)}) fusion(f32[2,4096]{1,0:T(2,128)S(1)} %copy-done.6, f32[2,4096]{1,0:T(2,128)S(1)} %copy-done.8, pred[2,128]{1,0:T(4,128)(4,1)} %copy-done.11, bf16[2,64,4096]{2,1,0:T(8,128)(2,1)} %copy-done.2, bf16[2,64,4096]{2,1,0:T(8,128)(2,1)S(1)} %maximum_select_fusion.1, ...), kind=kOutput, calls=%fused_computation.9 | convolution fusion | flops 427065088 | bytes 13796609 | tf_op jit(solution)/shard_map/cth,cdh->ctd/dot_general | solution.py:124
  135.9 1.5 collective-permute-start.6
  137.5 43.5 %collective-permute-done.6 = f32[2,64,4096]{2,1,0:T(8,128)S(1)} collective-permute-done((f32[2,64,4096]{2,1,0:T(8,128)S(1)}, f32[2,64,4096]{2,1,0:T(8,128)S(1)}, u32[]{:S(2)}, u32[]{:S(2)}) %collective-permute-start.6) | collective-permute-done | bytes 2097184 | tf_op jit(solution)/shard_map/ppermute | solution.py:14
  181.7 2.6 %collective-permute-done.7 = f32[2,32,4096]{2,1,0:T(8,128)S(1)} collective-permute-done((f32[2,32,4096]{2,1,0:T(8,128)S(1)}, f32[2,32,4096]{2,1,0:T(8,128)S(1)}, u32[]{:S(2)}, u32[]{:S(2)}) %collective-permute-start.7) | collective-permute-done | bytes 1048608 | tf_op jit(solution)/shard_map/ppermute | solution.py:14
  185.6 1.5 collective-permute-start.8
  187.7 1.6 collective-permute-done.8
  190.6 10.0 %all-reduce = f32[2,32,4]{1,0,2:T(2,128)S(1)} all-reduce(f32[2,32,4]{1,0,2:T(2,128)S(1)} %select_add_fusion.2), channel_id=6, replica_groups=mesh['section'=8,'tensor'=4] {'tensor'}, use_global_device_ids=true, to_apply=%region_8.9.clone | all-reduce | flops 256 | bytes 2048
  201.2 10.7 %reduce-scatter.8.cloned.1.call-done = f32[2,32,1024]{2,1,0:T(8,128)} async-done(((f32[2,32,4096]{2,1,0:T(8,128)}), f32[2,32,1024]{2,1,0:T(8,128)}) %reduce-scatter.8.cloned.1.call-update) | async-done | bytes 262160 | tf_op jit(solution)/shard_map/reduce_scatter | solution.py:24
  212.0 1.2 fusion.32
  213.2 1.5 collective-permute-start.10
  214.8 3.5 %collective-permute-done.10 = bf16[2,32,1024]{2,1,0:T(8,128)(2,1)S(1)} collective-permute-done((bf16[2,32,1024]{2,1,0:T(8,128)(2,1)S(1)}, bf16[2,32,1024]{2,1,0:T(8,128)(2,1)S(1)}, u32[]{:S(2)}, u32[]{:S(2)}) %collective-permute-start.10) | collective-permute-done | bytes 131104 | tf_op jit(solution)/shard_map/ppermute | solution.py:19
  (80 shorter events, 15.5 us)
Async XLA Ops:
  6.5 81.9 %copy-start = (bf16[1,2,128,128]{3,2,1,0:T(8,128)(2,1)S(1)}, bf16[1,2,128,128]{3,2,1,0:T(8,128)(2,1)}, u32[]{:S(2)}) copy-start(bf16[1,2,128,128]{3,2,1,0:T(8,128)(2,1)} %param.10) | copy-start | bytes 196612
  6.5 50.4 %copy-start.12 = (bf16[1,2,4096,32]{2,3,1,0:T(8,128)(2,1)S(1)}, bf16[1,2,4096,32]{2,3,1,0:T(8,128)(2,1)}, u32[]{:S(2)}) copy-start(bf16[1,2,4096,32]{2,3,1,0:T(8,128)(2,1)} %param.14) | copy-start | bytes 1572868
  6.5 102.9 %reduce-scatter.6.cloned.1.call-start = ((), (), s32[]{:S(2)}) async-start(), calls=%async_computation.4 | async-start | bytes 163840 | tf_op jit(solution)/shard_map/reduce_scatter | solution.py:25
  7.3 18.2 %collective-permute-start.2 = (bf16[2,32]{1,0:T(2,128)(2,1)S(1)}, bf16[2,32]{1,0:T(2,128)(2,1)S(1)}, u32[]{:S(2)}, u32[]{:S(2)}) collective-permute-start(bf16[2,32]{1,0:T(2,128)(2,1)S(1)} %convert_bitcast_fusion), channel_id=1, source_target_pairs={{0,4},{4,0},{8,12},{12,8},{16,20},{20,16},{24,28},{28,24},{1,5},{5... | collective-permute-start | bytes 392 | tf_op jit(solution)/shard_map/ppermute | solution.py:14
  7.8 19.3 %collective-permute-start.4 = (bf16[2,2,1024]{2,1,0:T(2,128)(2,1)}, bf16[2,2,1024]{2,1,0:T(2,128)(2,1)S(1)}, u32[]{:S(2)}, u32[]{:S(2)}) collective-permute-start(bf16[2,2,1024]{2,1,0:T(2,128)(2,1)} %bitcast.58), channel_id=1, source_target_pairs={{0,4},{4,0},{8,12},{12,8},{16,20},{20,16},{24,28},{28,24},{1,5},{5... | collective-permute-start | bytes 24584 | tf_op jit(solution)/shard_map/ppermute | solution.py:14
  25.5 6.3 %collective-permute-start = (bf16[2,32,4096]{2,1,0:T(8,128)(2,1)S(1)}, bf16[2,32,4096]{2,1,0:T(8,128)(2,1)S(1)}, u32[]{:S(2)}, u32[]{:S(2)}) collective-permute-start(bf16[2,32,4096]{2,1,0:T(8,128)(2,1)S(1)} %bitcast.52), channel_id=1, source_target_pairs={{0,4},{4,0},{8,12},{12,8},{16,20},{20,16},{24,28},{28,24},{1,5},{5... | collective-permute-start | bytes 1572872 | tf_op jit(solution)/shard_map/ppermute | solution.py:14
  25.6 3.6 %collective-permute-start.3 = (bf16[2,64]{1,0:T(2,128)(2,1)S(1)}, bf16[2,64]{1,0:T(2,128)(2,1)S(1)}, u32[]{:S(2)}, u32[]{:S(2)}) collective-permute-start(bf16[2,64]{1,0:T(2,128)(2,1)S(1)} %broadcast_select_fusion.6), channel_id=1, source_target_pairs={{0,8},{4,12},{8,0},{12,4},{16,24},{20,28},{24,16},{28,20},{1,9},{5... | collective-permute-start | bytes 776 | tf_op jit(solution)/shard_map/ppermute | solution.py:14
  27.9 3.8 %collective-permute-start.5 = (bf16[2,2,2048]{2,1,0:T(2,128)(2,1)S(1)}, bf16[2,2,2048]{2,1,0:T(2,128)(2,1)S(1)}, u32[]{:S(2)}, u32[]{:S(2)}) collective-permute-start(bf16[2,2,2048]{2,1,0:T(2,128)(2,1)S(1)} %broadcast_select_fusion.2), channel_id=1, source_target_pairs={{0,8},{4,12},{8,0},{12,4},{16,24},{20,28},{24,16},{28,20},{1,9},{5... | collective-permute-start | bytes 49160 | tf_op jit(solution)/shard_map/ppermute | solution.py:14
  29.2 56.9 %copy-start.11 = (pred[2,128]{1,0:T(4,128)(4,1)}, pred[2,128]{1,0:T(4,128)(4,1)S(1)}, u32[]{:S(2)}) copy-start(pred[2,128]{1,0:T(4,128)(4,1)S(1)} %fusion.52) | copy-start | bytes 772
  32.0 24.2 %collective-permute-start.1 = (bf16[2,64,4096]{2,1,0:T(8,128)(2,1)S(1)}, bf16[2,64,4096]{2,1,0:T(8,128)(2,1)S(1)}, u32[]{:S(2)}, u32[]{:S(2)}) collective-permute-start(bf16[2,64,4096]{2,1,0:T(8,128)(2,1)S(1)} %maximum_select_fusion.1), channel_id=1, source_target_pairs={{0,8},{4,12},{8,0},{12,4},{16,24},{20,28},{24,16},{28,20},{1,9},{5... | collective-permute-start | bytes 3145736 | tf_op jit(solution)/shard_map/ppermute | solution.py:14
  32.7 53.5 %copy-start.5 = (f32[2,4096]{1,0:T(2,128)}, f32[2,4096]{1,0:T(2,128)S(1)}, u32[]{:S(2)}) copy-start(f32[2,4096]{1,0:T(2,128)S(1)} %get-tuple-element.16) | copy-start | bytes 98308
  32.7 53.5 %copy-start.7 = (f32[2,4096]{1,0:T(2,128)}, f32[2,4096]{1,0:T(2,128)S(1)}, u32[]{:S(2)}) copy-start(f32[2,4096]{1,0:T(2,128)S(1)} %get-tuple-element.17) | copy-start | bytes 98308
  56.2 30.0 %copy-start.2 = (bf16[2,64,4096]{2,1,0:T(8,128)(2,1)}, bf16[2,64,4096]{2,1,0:T(8,128)(2,1)S(1)}, u32[]{:S(2)}) copy-start(bf16[2,64,4096]{2,1,0:T(8,128)(2,1)S(1)} %collective-permute-done.1) | copy-start | bytes 3145732
  89.4 40.0 %reduce-scatter.4.cloned.1.call-start = ((), (), s32[]{:S(2)}) async-start(), calls=%async_computation.3 | async-start | bytes 163840 | tf_op jit(solution)/shard_map/reduce_scatter | solution.py:24
  89.6 40.5 %copy-start.6 = (f32[2,4096]{1,0:T(2,128)S(1)}, f32[2,4096]{1,0:T(2,128)}, u32[]{:S(2)}) copy-start(f32[2,4096]{1,0:T(2,128)} %copy-done.5) | copy-start | bytes 98308
  89.6 40.5 %copy-start.8 = (f32[2,4096]{1,0:T(2,128)S(1)}, f32[2,4096]{1,0:T(2,128)}, u32[]{:S(2)}) copy-start(f32[2,4096]{1,0:T(2,128)} %copy-done.7) | copy-start | bytes 98308
  91.5 120.5 %reduce-scatter.8.cloned.1.call-start = ((), (), s32[]{:S(2)}) async-start(), calls=%async_computation.5 | async-start | bytes 1310720 | tf_op jit(solution)/shard_map/reduce_scatter | solution.py:24
  135.9 45.1 %collective-permute-start.6 = (f32[2,64,4096]{2,1,0:T(8,128)S(1)}, f32[2,64,4096]{2,1,0:T(8,128)S(1)}, u32[]{:S(2)}, u32[]{:S(2)}) collective-permute-start(f32[2,64,4096]{2,1,0:T(8,128)S(1)} %slice_select_fusion), channel_id=1, source_target_pairs={{0,8},{4,12},{8,0},{12,4},{16,24},{20,28},{24,16},{28,20},{1,9},{5... | collective-permute-start | bytes 6291464 | tf_op jit(solution)/shard_map/ppermute | solution.py:14
  181.6 30.4 %copy-start.3 = (bf16[1,2,32,1024]{3,2,1,0:T(8,128)(2,1)S(1)}, bf16[1,2,32,1024]{3,2,1,0:T(8,128)(2,1)}, u32[]{:S(2)}) copy-start(bf16[1,2,32,1024]{3,2,1,0:T(8,128)(2,1)} %param.8) | copy-start | bytes 393220
  181.6 30.4 %copy-start.4 = (bf16[1,2,32,1024]{3,2,1,0:T(8,128)(2,1)S(1)}, bf16[1,2,32,1024]{3,2,1,0:T(8,128)(2,1)}, u32[]{:S(2)}) copy-start(bf16[1,2,32,1024]{3,2,1,0:T(8,128)(2,1)} %param.9) | copy-start | bytes 393220
  181.6 2.7 %collective-permute-start.7 = (f32[2,32,4096]{2,1,0:T(8,128)S(1)}, f32[2,32,4096]{2,1,0:T(8,128)S(1)}, u32[]{:S(2)}, u32[]{:S(2)}) collective-permute-start(f32[2,32,4096]{2,1,0:T(8,128)S(1)} %slice_select_fusion.1), channel_id=1, source_target_pairs={{0,4},{4,0},{8,12},{12,8},{16,20},{20,16},{24,28},{28,24},{1,5},{5... | collective-permute-start | bytes 3145736 | tf_op jit(solution)/shard_map/ppermute | solution.py:14
  185.6 3.6 %collective-permute-start.8 = (f32[2,64,4]{1,0,2:T(2,128)S(1)}, f32[2,64,4]{1,0,2:T(2,128)S(1)}, u32[]{:S(2)}, u32[]{:S(2)}) collective-permute-start(f32[2,64,4]{1,0,2:T(2,128)S(1)} %broadcast_in_dim.67), channel_id=1, source_target_pairs={{0,8},{4,12},{8,0},{12,4},{16,24},{20,28},{24,16},{28,20},{1,9},{5... | collective-permute-start | bytes 6152 | tf_op jit(solution)/shard_map/ppermute | solution.py:14
  189.3 1.2 collective-permute-start.9
  213.2 5.0 %collective-permute-start.10 = (bf16[2,32,1024]{2,1,0:T(8,128)(2,1)S(1)}, bf16[2,32,1024]{2,1,0:T(8,128)(2,1)S(1)}, u32[]{:S(2)}, u32[]{:S(2)}) collective-permute-start(bf16[2,32,1024]{2,1,0:T(8,128)(2,1)S(1)} %fusion.32), channel_id=1, source_target_pairs={{0,16},{4,20},{8,24},{12,28},{16,0},{20,4},{24,8},{28,12},{1,17},{... | collective-permute-start | bytes 393224 | tf_op jit(solution)/shard_map/ppermute | solution.py:19
  (5 other events, 71.8 us)
Sparse Core Ops, SparseCore 0:
  89.5 19.9 reduce-scatter.5
  111.7 17.5 reduce-scatter.3
  185.7 26.2 reduce-scatter.7
where the time goes:
time: 226 us; the launch traced here: 225 us
  waiting for transfers between devices  123 us (54%)
  blocking collectives  54.3 us (24%)
  matrix products  13.8 us (6%)
  between operations  13.4 us (6%)
  other arithmetic  9.83 us (4%)
  starting transfers between devices  7.91 us (4%)
  local copies, waits for them, and re-layouts  3.58 us (2%)
    ppermute x10, waiting for transfers between devices, swapped(): return lax.ppermute(value, axis, pairs)  75.4 us
    reduce_scatter x2, waiting for transfers between devices, sum_columns(): lax.psum_scatter(first, 'tensor', scatter_dimension=2, tiled=True)  29.9 us
    all_gather x1, blocking collectives, per_device(): x_cols = lax.all_gather(x_local, 'tensor', axis=2, tiled=True)  17.7 us
    reduce_scatter x1, waiting for transfers between devices, sum_columns(): lax.psum_scatter(second, 'tensor', scatter_dimension=2, tiled=True)  13.9 us
    all_gather x1, blocking collectives, per_device(): lax.all_gather(key_part, 'tensor', axis=2, tiled=True)  13.4 us
    all_gather x1, blocking collectives, per_device(): lax.all_gather(value_part, 'tensor', axis=2, tiled=True)  13.2 us
    unnamed x1, blocking collectives  10 us
    ppermute x10, starting transfers between devices, swapped(): return lax.ppermute(value, axis, pairs)  6.29 us
  transfers between devices with their start and end apart: 14, of which 11 were waited for; matrix products, arithmetic and copies ran while one was open for 4% of the time, Pallas kernels for 0%

commit v1 on v0

--- a/solution.py
+++ b/solution.py
@@ -6,6 +6,18 @@
 HEAD_DIM = 128
 SUB = 4
 epsilon = 1e-05
+
+
+def gather_by_bits(x, axis, dim):
+    ways, here, lap = (lax.axis_size(axis), lax.axis_index(axis), x.shape[dim])
+    line, have = (x, 1)
+    while have < ways:
+        line = jnp.concatenate(
+            [line, lax.ppermute(line, axis, [(d, (d - have) % ways) for d in range(ways)])],
+            axis=dim,
+        )
+        have = 2 * have
+    return jnp.roll(line, here * lap, axis=dim)
 
 
 def swapped(value, axis, stride):
@@ -90,7 +102,7 @@
     ).astype(jnp.bfloat16)
     key_rows, value_rows = (
         lax.all_gather(key_part, "tensor", axis=2, tiled=True),
-        lax.all_gather(value_part, "tensor", axis=2, tiled=True),
+        gather_by_bits(value_part, "tensor", 2),
     )
     softmax_scale = HEAD_DIM ** (-0.5)
     scores = (

time: 226 us -> 215 us (0.951)
  blocking collectives: 54.3 us -> 41.1 us
  waiting for transfers between devices: 123 us -> 114 us
  starting transfers between devices: 7.91 us -> 12.6 us
  local copies, waits for them, and re-layouts: 3.58 us -> 7.93 us
    all_gather x1 -> x0, blocking collectives: 13.2 us -> none  [per_device(): lax.all_gather(value_part, 'tensor', axis=2, tiled=True)]
    reduce_scatter x1, waiting for transfers between devices: 13.9 us -> 2.23 us  [sum_columns(): lax.psum_scatter(second, 'tensor', scatter_dimension=2, tiled=True)]
    ppermute x0 -> x2, starting transfers between devices: none -> 4.74 us  [gather_by_bits(): lax.ppermute(line, axis, [(d, (d - have) % ways) for d in range(ways)])]
    unnamed x34 -> x40, local copies, waits for them, and re-layouts: 3.52 us -> 7.26 us
    ppermute x0 -> x2, waiting for transfers between devices: none -> 3.32 us  [gather_by_bits(): lax.ppermute(line, axis, [(d, (d - have) % ways) for d in range(ways)])]
  transfers between devices with their start and end apart: 14 -> 16, of which waited for: 11 -> 12; matrix products, arithmetic and copies ran while one was open for 4% -> 7% of each run, Pallas kernels for 0% -> 0%
where the time goes in v1:
time: 215 us
  waiting for transfers between devices  114 us (53%)
  blocking collectives  41.1 us (19%)
  matrix products  14.7 us (7%)
  between operations  13.4 us (6%)
  starting transfers between devices  12.6 us (6%)
  other arithmetic  10.5 us (5%)
  local copies, waits for them, and re-layouts  7.93 us (4%)
    ppermute x10, waiting for transfers between devices, swapped(): return lax.ppermute(value, axis, pairs)  75.4 us
    reduce_scatter x2, waiting for transfers between devices, sum_columns(): lax.psum_scatter(first, 'tensor', scatter_dimension=2, tiled=True)  30 us
    all_gather x1, blocking collectives, per_device(): x_cols = lax.all_gather(x_local, 'tensor', axis=2, tiled=True)  17.7 us
    all_gather x1, blocking collectives, per_device(): lax.all_gather(key_part, 'tensor', axis=2, tiled=True)  13.4 us
    unnamed x1, blocking collectives  10 us
    unnamed x40, local copies, waits for them, and re-layouts  7.26 us
    ppermute x10, starting transfers between devices, swapped(): return lax.ppermute(value, axis, pairs)  6.3 us
    dot_general x1, matrix products, per_device(): jnp.einsum('cth,cdh->ctd', joined_grads, joined_weights, preferred_elemen...  5.48 us
  transfers between devices with their start and end apart: 16, of which 12 were waited for; matrix products, arithmetic and copies ran while one was open for 7% of the time, Pallas kernels for 0%

profile of v1, /device:TPU:0, one launch (start us, length us, event | category | flops | bytes accessed | tf_op | source)
XLA Modules:
  0.0 214.8 jit_solution(2440480266309203986)
XLA Ops:
  7.8 17.7 %all-gather = bf16[1,2,32,4096]{3,2,1,0:T(8,128)(2,1)S(1)} all-gather(bf16[1,2,32,1024]{3,2,1,0:T(8,128)(2,1)} %param.8), channel_id=2, replica_groups=mesh['section'=8,'tensor'=4] {'tensor'}, dimensions={3}, use_global_device_ids=true | all-gather | bytes 655360 | tf_op jit(solution)/shard_map/all_gather | solution.py:82
  25.6 1.5 collective-permute-start.3
  29.2 2.4 %collective-permute-done.5 = bf16[2,2,2048]{2,1,0:T(2,128)(2,1)S(1)} collective-permute-done((bf16[2,2,2048]{2,1,0:T(2,128)(2,1)S(1)}, bf16[2,2,2048]{2,1,0:T(2,128)(2,1)S(1)}, u32[]{:S(2)}, u32[]{:S(2)}) %collective-permute-start.5) | collective-permute-done | bytes 16416 | tf_op jit(solution)/shard_map/ppermute | solution.py:26
  32.7 23.5 %collective-permute-done.1 = bf16[2,64,4096]{2,1,0:T(8,128)(2,1)S(1)} collective-permute-done((bf16[2,64,4096]{2,1,0:T(8,128)(2,1)S(1)}, bf16[2,64,4096]{2,1,0:T(8,128)(2,1)S(1)}, u32[]{:S(2)}, u32[]{:S(2)}) %collective-permute-start.1) | collective-permute-done | bytes 1048608 | tf_op jit(solution)/shard_map/ppermute | solution.py:26
  58.2 13.4 %all_gather.7 = bf16[2,128,128]{1,2,0:T(8,128)(2,1)S(1)} all-gather(bf16[2,128,32]{1,2,0:T(8,128)(2,1)S(1)} %convolution_convert_fusion.2), channel_id=1, replica_groups=mesh['section'=8,'tensor'=4] {'tensor'}, dimensions={2}, use_global_device_ids=true | all-gather | bytes 81920 | tf_op jit(solution)/shard_map/all_gather | solution.py:104
  71.7 1.4 fusion.22
  74.6 1.9 constant_dynamic-update-slice_fusion.5
  76.5 3.8 %collective-permute-start.6 = (bf16[2,128,32]{1,2,0:T(8,128)(2,1)}, bf16[2,128,32]{1,2,0:T(8,128)(2,1)S(1)}, u32[]{:S(2)}, u32[]{:S(2)}) collective-permute-start(bf16[2,128,32]{1,2,0:T(8,128)(2,1)} %get-tuple-element.16), channel_id=1, source_target_pairs={{0,3},{1,0},{2,1},{3,2},{4,7},{5,4},{6,5},{7,6},{8,11},{9,8},{10,9... | collective-permute-start | bytes 49160 | tf_op jit(solution)/shard_map/ppermute | solution.py:16
  80.3 1.5 fusion.43
  84.2 3.3 %collective-permute-done.7 = bf16[2,128,64]{1,2,0:T(8,128)(2,1)S(1)} collective-permute-done((bf16[2,128,64]{1,2,0:T(8,128)(2,1)S(1)}, bf16[2,128,64]{1,2,0:T(8,128)(2,1)S(1)}, u32[]{:S(2)}, u32[]{:S(2)}) %collective-permute-start.7) | collective-permute-done | bytes 32800 | tf_op jit(solution)/shard_map/ppermute | solution.py:16
  91.7 1.7 fusion.25
  93.6 2.8 %copy.12 = bf16[1,2,4096,128]{2,3,1,0:T(8,128)(2,1)} copy(bf16[1,2,4096,128]{3,2,1,0:T(8,128)(2,1)S(1)} %copy-done.1) | data formatting | bytes 4194304 | tf_op args[5]
  96.5 2.2 %reduce-scatter.6.cloned.1.call-done = f32[2,128,32]{1,2,0:T(8,128)} async-done(((f32[2,128,128]{1,2,0:T(8,128)}), f32[2,128,32]{1,2,0:T(8,128)}) %reduce-scatter.6.cloned.1.call-update) | async-done | bytes 32784 | tf_op jit(solution)/shard_map/reduce_scatter | solution.py:37
  99.5 19.1 %reduce-scatter.4.cloned.1.call-done = f32[2,128,32]{1,2,0:T(8,128)} async-done(((f32[2,128,128]{1,2,0:T(8,128)}), f32[2,128,32]{1,2,0:T(8,128)}) %reduce-scatter.4.cloned.1.call-update) | async-done | bytes 32784 | tf_op jit(solution)/shard_map/reduce_scatter | solution.py:36
  119.4 5.5 %fusion.6 = (f32[2,128]{1,0:T(2,128)S(1)}, f32[2,128,4096]{2,1,0:T(8,128)}, f32[2,128,4096]{2,1,0:T(8,128)S(1)}) fusion(f32[2,4096]{1,0:T(2,128)} %copy-done.6, f32[2,4096]{1,0:T(2,128)} %copy-done.7, pred[2,128]{1,0:T(4,128)(4,1)S(1)} %copy-done.12, bf16[2,64,4096]{2,1,0:T(8,128)(2,1)} %copy-done.2, bf16[2,64,4096]{2,1,0:T(8,128)(2,1)S(1)} %maximum_select_fusion.1, ...), kind=kOutput, calls=%fused_computation.9 | convolution fusion | flops 427065088 | bytes 13796609 | tf_op jit(solution)/shard_map/cth,cdh->ctd/dot_general | solution.py:136
  125.2 1.5 collective-permute-start.8
  126.7 43.5 %collective-permute-done.8 = f32[2,64,4096]{2,1,0:T(8,128)S(1)} collective-permute-done((f32[2,64,4096]{2,1,0:T(8,128)S(1)}, f32[2,64,4096]{2,1,0:T(8,128)S(1)}, u32[]{:S(2)}, u32[]{:S(2)}) %collective-permute-start.8) | collective-permute-done | bytes 2097184 | tf_op jit(solution)/shard_map/ppermute | solution.py:26
  170.9 2.6 %collective-permute-done.9 = f32[2,32,4096]{2,1,0:T(8,128)S(1)} collective-permute-done((f32[2,32,4096]{2,1,0:T(8,128)S(1)}, f32[2,32,4096]{2,1,0:T(8,128)S(1)}, u32[]{:S(2)}, u32[]{:S(2)}) %collective-permute-start.9) | collective-permute-done | bytes 1048608 | tf_op jit(solution)/shard_map/ppermute | solution.py:26
  174.9 1.5 collective-permute-start.10
  177.0 1.5 collective-permute-done.10
  179.8 10.0 %all-reduce = f32[2,32,4]{1,0,2:T(2,128)S(1)} all-reduce(f32[2,32,4]{1,0,2:T(2,128)S(1)} %select_add_fusion.2), channel_id=6, replica_groups=mesh['section'=8,'tensor'=4] {'tensor'}, use_global_device_ids=true, to_apply=%region_8.9.clone | all-reduce | flops 256 | bytes 2048
  190.5 10.8 %reduce-scatter.8.cloned.1.call-done = f32[2,32,1024]{2,1,0:T(8,128)} async-done(((f32[2,32,4096]{2,1,0:T(8,128)}), f32[2,32,1024]{2,1,0:T(8,128)}) %reduce-scatter.8.cloned.1.call-update) | async-done | bytes 262160 | tf_op jit(solution)/shard_map/reduce_scatter | solution.py:36
  202.6 1.5 collective-permute-start.12
  204.1 3.5 %collective-permute-done.12 = bf16[2,32,1024]{2,1,0:T(8,128)(2,1)S(1)} collective-permute-done((bf16[2,32,1024]{2,1,0:T(8,128)(2,1)S(1)}, bf16[2,32,1024]{2,1,0:T(8,128)(2,1)S(1)}, u32[]{:S(2)}, u32[]{:S(2)}) %collective-permute-start.12) | collective-permute-done | bytes 131104 | tf_op jit(solution)/shard_map/ppermute | solution.py:31
  (91 shorter events, 23.0 us)
Async XLA Ops:
  6.5 73.8 %copy-start = (bf16[1,2,128,128]{3,2,1,0:T(8,128)(2,1)S(1)}, bf16[1,2,128,128]{3,2,1,0:T(8,128)(2,1)}, u32[]{:S(2)}) copy-start(bf16[1,2,128,128]{3,2,1,0:T(8,128)(2,1)} %param.10) | copy-start | bytes 196612
  6.5 92.2 %reduce-scatter.6.cloned.1.call-start = ((), (), s32[]{:S(2)}) async-start(), calls=%async_computation.4 | async-start | bytes 163840 | tf_op jit(solution)/shard_map/reduce_scatter | solution.py:37
  7.3 18.2 %collective-permute-start.2 = (bf16[2,32]{1,0:T(2,128)(2,1)S(1)}, bf16[2,32]{1,0:T(2,128)(2,1)S(1)}, u32[]{:S(2)}, u32[]{:S(2)}) collective-permute-start(bf16[2,32]{1,0:T(2,128)(2,1)S(1)} %convert_bitcast_fusion), channel_id=1, source_target_pairs={{0,4},{4,0},{8,12},{12,8},{16,20},{20,16},{24,28},{28,24},{1,5},{5... | collective-permute-start | bytes 392 | tf_op jit(solution)/shard_map/ppermute | solution.py:26
  7.7 19.3 %collective-permute-start.4 = (bf16[2,2,1024]{2,1,0:T(2,128)(2,1)}, bf16[2,2,1024]{2,1,0:T(2,128)(2,1)S(1)}, u32[]{:S(2)}, u32[]{:S(2)}) collective-permute-start(bf16[2,2,1024]{2,1,0:T(2,128)(2,1)} %bitcast.59), channel_id=1, source_target_pairs={{0,4},{4,0},{8,12},{12,8},{16,20},{20,16},{24,28},{28,24},{1,5},{5... | collective-permute-start | bytes 24584 | tf_op jit(solution)/shard_map/ppermute | solution.py:26
  25.4 6.3 %collective-permute-start = (bf16[2,32,4096]{2,1,0:T(8,128)(2,1)S(1)}, bf16[2,32,4096]{2,1,0:T(8,128)(2,1)S(1)}, u32[]{:S(2)}, u32[]{:S(2)}) collective-permute-start(bf16[2,32,4096]{2,1,0:T(8,128)(2,1)S(1)} %bitcast.53), channel_id=1, source_target_pairs={{0,4},{4,0},{8,12},{12,8},{16,20},{20,16},{24,28},{28,24},{1,5},{5... | collective-permute-start | bytes 1572872 | tf_op jit(solution)/shard_map/ppermute | solution.py:26
  25.5 31.5 %copy-start.13 = (bf16[1,2,4096,32]{2,3,1,0:T(8,128)(2,1)S(1)}, bf16[1,2,4096,32]{2,3,1,0:T(8,128)(2,1)}, u32[]{:S(2)}) copy-start(bf16[1,2,4096,32]{2,3,1,0:T(8,128)(2,1)} %param.14) | copy-start | bytes 1572868
  25.6 3.6 %collective-permute-start.3 = (bf16[2,64]{1,0:T(2,128)(2,1)S(1)}, bf16[2,64]{1,0:T(2,128)(2,1)S(1)}, u32[]{:S(2)}, u32[]{:S(2)}) collective-permute-start(bf16[2,64]{1,0:T(2,128)(2,1)S(1)} %broadcast_select_fusion.6), channel_id=1, source_target_pairs={{0,8},{4,12},{8,0},{12,4},{16,24},{20,28},{24,16},{28,20},{1,9},{5... | collective-permute-start | bytes 776 | tf_op jit(solution)/shard_map/ppermute | solution.py:26
  27.9 3.8 %collective-permute-start.5 = (bf16[2,2,2048]{2,1,0:T(2,128)(2,1)S(1)}, bf16[2,2,2048]{2,1,0:T(2,128)(2,1)S(1)}, u32[]{:S(2)}, u32[]{:S(2)}) collective-permute-start(bf16[2,2,2048]{2,1,0:T(2,128)(2,1)S(1)} %broadcast_select_fusion.2), channel_id=1, source_target_pairs={{0,8},{4,12},{8,0},{12,4},{16,24},{20,28},{24,16},{28,20},{1,9},{5... | collective-permute-start | bytes 49160 | tf_op jit(solution)/shard_map/ppermute | solution.py:26
  29.2 45.4 %copy-start.11 = (pred[2,128]{1,0:T(4,128)(4,1)}, pred[2,128]{1,0:T(4,128)(4,1)S(1)}, u32[]{:S(2)}) copy-start(pred[2,128]{1,0:T(4,128)(4,1)S(1)} %fusion.54) | copy-start | bytes 772
  31.9 24.2 %collective-permute-start.1 = (bf16[2,64,4096]{2,1,0:T(8,128)(2,1)S(1)}, bf16[2,64,4096]{2,1,0:T(8,128)(2,1)S(1)}, u32[]{:S(2)}, u32[]{:S(2)}) collective-permute-start(bf16[2,64,4096]{2,1,0:T(8,128)(2,1)S(1)} %maximum_select_fusion.1), channel_id=1, source_target_pairs={{0,8},{4,12},{8,0},{12,4},{16,24},{20,28},{24,16},{28,20},{1,9},{5... | collective-permute-start | bytes 3145736 | tf_op jit(solution)/shard_map/ppermute | solution.py:26
  32.7 41.9 %copy-start.6 = (f32[2,4096]{1,0:T(2,128)}, f32[2,4096]{1,0:T(2,128)S(1)}, u32[]{:S(2)}) copy-start(f32[2,4096]{1,0:T(2,128)S(1)} %get-tuple-element.18) | copy-start | bytes 98308
  32.7 41.9 %copy-start.7 = (f32[2,4096]{1,0:T(2,128)}, f32[2,4096]{1,0:T(2,128)S(1)}, u32[]{:S(2)}) copy-start(f32[2,4096]{1,0:T(2,128)S(1)} %get-tuple-element.19) | copy-start | bytes 98308
  76.5 5.5 %collective-permute-start.6 = (bf16[2,128,32]{1,2,0:T(8,128)(2,1)}, bf16[2,128,32]{1,2,0:T(8,128)(2,1)S(1)}, u32[]{:S(2)}, u32[]{:S(2)}) collective-permute-start(bf16[2,128,32]{1,2,0:T(8,128)(2,1)} %get-tuple-element.16), channel_id=1, source_target_pairs={{0,3},{1,0},{2,1},{3,2},{4,7},{5,4},{6,5},{7,6},{8,11},{9,8},{10,9... | collective-permute-start | bytes 49160 | tf_op jit(solution)/shard_map/ppermute | solution.py:16
  81.9 37.6 %copy-start.12 = (pred[2,128]{1,0:T(4,128)(4,1)S(1)}, pred[2,128]{1,0:T(4,128)(4,1)}, u32[]{:S(2)}) copy-start(pred[2,128]{1,0:T(4,128)(4,1)} %copy-done.11) | copy-start | bytes 772
  81.9 36.8 %reduce-scatter.4.cloned.1.call-start = ((), (), s32[]{:S(2)}) async-start(), calls=%async_computation.3 | async-start | bytes 163840 | tf_op jit(solution)/shard_map/reduce_scatter | solution.py:36
  82.7 4.8 %collective-permute-start.7 = (bf16[2,128,64]{1,2,0:T(8,128)(2,1)S(1)}, bf16[2,128,64]{1,2,0:T(8,128)(2,1)S(1)}, u32[]{:S(2)}, u32[]{:S(2)}) collective-permute-start(bf16[2,128,64]{1,2,0:T(8,128)(2,1)S(1)} %pad_maximum_fusion), channel_id=1, source_target_pairs={{0,2},{1,3},{2,0},{3,1},{4,6},{5,7},{6,4},{7,5},{8,10},{9,11},{10,... | collective-permute-start | bytes 98312 | tf_op jit(solution)/shard_map/ppermute | solution.py:16
  93.5 107.9 %reduce-scatter.8.cloned.1.call-start = ((), (), s32[]{:S(2)}) async-start(), calls=%async_computation.5 | async-start | bytes 1310720 | tf_op jit(solution)/shard_map/reduce_scatter | solution.py:36
  125.2 45.1 %collective-permute-start.8 = (f32[2,64,4096]{2,1,0:T(8,128)S(1)}, f32[2,64,4096]{2,1,0:T(8,128)S(1)}, u32[]{:S(2)}, u32[]{:S(2)}) collective-permute-start(f32[2,64,4096]{2,1,0:T(8,128)S(1)} %slice_select_fusion), channel_id=1, source_target_pairs={{0,8},{4,12},{8,0},{12,4},{16,24},{20,28},{24,16},{28,20},{1,9},{5... | collective-permute-start | bytes 6291464 | tf_op jit(solution)/shard_map/ppermute | solution.py:26
  170.8 30.5 %copy-start.3 = (bf16[1,2,32,1024]{3,2,1,0:T(8,128)(2,1)S(1)}, bf16[1,2,32,1024]{3,2,1,0:T(8,128)(2,1)}, u32[]{:S(2)}) copy-start(bf16[1,2,32,1024]{3,2,1,0:T(8,128)(2,1)} %param.8) | copy-start | bytes 393220
  170.9 30.5 %copy-start.4 = (bf16[1,2,32,1024]{3,2,1,0:T(8,128)(2,1)S(1)}, bf16[1,2,32,1024]{3,2,1,0:T(8,128)(2,1)}, u32[]{:S(2)}) copy-start(bf16[1,2,32,1024]{3,2,1,0:T(8,128)(2,1)} %param.9) | copy-start | bytes 393220
  170.9 2.7 %collective-permute-start.9 = (f32[2,32,4096]{2,1,0:T(8,128)S(1)}, f32[2,32,4096]{2,1,0:T(8,128)S(1)}, u32[]{:S(2)}, u32[]{:S(2)}) collective-permute-start(f32[2,32,4096]{2,1,0:T(8,128)S(1)} %slice_select_fusion.1), channel_id=1, source_target_pairs={{0,4},{4,0},{8,12},{12,8},{16,20},{20,16},{24,28},{28,24},{1,5},{5... | collective-permute-start | bytes 3145736 | tf_op jit(solution)/shard_map/ppermute | solution.py:26
  174.9 3.6 %collective-permute-start.10 = (f32[2,64,4]{1,0,2:T(2,128)S(1)}, f32[2,64,4]{1,0,2:T(2,128)S(1)}, u32[]{:S(2)}, u32[]{:S(2)}) collective-permute-start(f32[2,64,4]{1,0,2:T(2,128)S(1)} %broadcast_in_dim.67), channel_id=1, source_target_pairs={{0,8},{4,12},{8,0},{12,4},{16,24},{20,28},{24,16},{28,20},{1,9},{5... | collective-permute-start | bytes 6152 | tf_op jit(solution)/shard_map/ppermute | solution.py:26
  178.6 1.2 collective-permute-start.11
  202.6 5.0 %collective-permute-start.12 = (bf16[2,32,1024]{2,1,0:T(8,128)(2,1)S(1)}, bf16[2,32,1024]{2,1,0:T(8,128)(2,1)S(1)}, u32[]{:S(2)}, u32[]{:S(2)}) collective-permute-start(bf16[2,32,1024]{2,1,0:T(8,128)(2,1)S(1)} %fusion.32), channel_id=1, source_target_pairs={{0,16},{4,20},{8,24},{12,28},{16,0},{20,4},{24,8},{28,12},{1,17},{... | collective-permute-start | bytes 393224 | tf_op jit(solution)/shard_map/ppermute | solution.py:31
  (8 other events, 82.2 us)
Sparse Core Ops, SparseCore 0:
  82.0 16.7 reduce-scatter.5
  101.0 17.6 reduce-scatter.3
  174.9 26.3 reduce-scatter.7
